TPU v7x, 128 devices: a whole 4x4x4 slice. The times are simulated.
128 devices in a mesh: blk: 4 (over x), tok: 32 (over y, z, core).
Axes of the slice: x: 4, y: 4, z: 4, core: 2. Of those that a mesh axis runs over, the one named last changes fastest.
Arguments:
- tokens: bfloat16 [32, 1024, 1664], P('tok', 'blk'), may hold values from -6 to 6
- segment_ids: int32 [32, 1024], P('tok'), may hold values from 0 to 31, as said below
- merge_index: int32 [32, 256, 4], P('tok'), may hold values from 0 to 1023, as said below
- segment_owner: int32 [32, 32], P('tok'), may hold values from 0 to 31, each once within a row
- ln1_gain: float32 [1664], replicated, may hold values from 0.1 to 1.9
- ln1_bias: float32 [1664], replicated, may hold values from -4 to 4
- w_qkv: bfloat16 [3, 1664, 1664], P(None, 'tok', 'blk'), may hold values from -0.15625 to 0.15625
- qkv_bias: float32 [3, 1664], P(None, 'blk'), may hold values from -6 to 6
- w_out: bfloat16 [1664, 1664], P('blk', 'tok'), may hold values from -0.15625 to 0.15625
- out_bias: float32 [1664], replicated, may hold values from -6 to 6
- ln2_gain: float32 [1664], replicated, may hold values from 0.1 to 1.9
- ln2_bias: float32 [1664], replicated, may hold values from -4 to 4
- w_fc1: bfloat16 [1664, 8192], P(None, 'blk'), may hold values from -0.15625 to 0.15625
- fc1_bias: float32 [8192], P('blk'), may hold values from -6 to 6
- w_fc2: bfloat16 [8192, 1664], P('blk'), may hold values from -0.0625 to 0.0625
- fc2_bias: float32 [1664], replicated, may hold values from -6 to 6
- ln3_gain: float32 [1664], replicated, may hold values from 0.1 to 1.9
- ln3_bias: float32 [1664], replicated, may hold values from -4 to 4
- w_proj: bfloat16 [6656, 1664], P('tok', 'blk'), may hold values from -0.078125 to 0.078125
- proj_bias: float32 [1664], P('blk'), may hold values from -6 to 6
Outputs:
- returned: bfloat16 [32, 32, 16, 1664], P('tok', None, None, 'blk')
Inputs may be any that keep to these rules, and one draw needn't show every extreme that they name: `segment_ids`: within a block each segment holds 4 to 64 tokens, one exactly 64; the four tokens of one row of merge_index share a segment. `merge_index`: the rows of one block name each token of the block exactly once. `segment_owner`: each block's row is a permutation of the owners.
All inputs are finite; a program needn't handle non-finite values.
Results may differ from a plain program's by a relative error of at most 0.015.
Values may be sent and summed in bfloat16 or wider, within the bound.
A program may use at most 128 MiB of HBM per device.

v0:
```python
import math
import jax
import jax.numpy as jnp
from jax import lax
from jax.sharding import PartitionSpec as P

HD = 104
EPS = 1e-06


def layer_norm(input_tensors, scales, offset):
    input_tensors = input_tensors.astype(jnp.float32)
    center = input_tensors - jnp.mean(input_tensors, axis=-1, keepdims=True)
    spread = jnp.mean(center * center, axis=-1, keepdims=True)
    return center * lax.rsqrt(spread + EPS) * scales + offset


def body(
    tokens,
    segment_ids,
    merge_index,
    segment_owner,
    ln1_gain,
    ln1_bias,
    w_qkv,
    qkv_bias,
    w_out,
    out_bias,
    ln2_gain,
    ln2_bias,
    w_fc1,
    fc1_bias,
    w_fc2,
    fc2_bias,
    ln3_gain,
    ln3_bias,
    w_proj,
    proj_bias,
):
    tok_block = tokens[0]
    row_count = tok_block.shape[0]
    model_width = tok_block.shape[1]
    head_cols = w_qkv.shape[2]
    heads_here = head_cols // HD
    normed_one = layer_norm(tok_block, ln1_gain, ln1_bias).astype(jnp.bfloat16)
    normed_all = lax.all_gather(normed_one, "blk", axis=0, tiled=True)
    all_rows = normed_all.shape[0]
    columns = normed_all
    projected_qkv = jnp.einsum(
        "td,cde->cte",
        columns,
        lax.all_gather(w_qkv, "tok", axis=1, tiled=True),
        preferred_element_type=jnp.float32,
    )
    projected_qkv = (projected_qkv + qkv_bias[:, None, :]).astype(jnp.bfloat16)
    projected_qkv = projected_qkv.reshape(3, all_rows, heads_here, HD)
    key_rows = projected_qkv[1]
    values = projected_qkv[2]
    segment_row = segment_ids[0]
    q_block = min(512, all_rows)
    block_count = all_rows // q_block
    query_rows = projected_qkv[0].reshape(block_count, q_block, heads_here, HD)
    query_segs = segment_row.reshape(block_count, q_block)
    score_scale = 1.0 / math.sqrt(HD)

    def attend(input_tensors):
        query_part, query_seg = input_tensors
        scores = (
            jnp.einsum("qhe,khe->hqk", query_part, key_rows, preferred_element_type=jnp.float32)
            * score_scale
        )
        allowed = query_seg[:, None] == segment_row[None, :]
        weights = jnp.where(allowed[None], jnp.exp(scores), 0.0)
        attn_probs = (weights / jnp.sum(weights, axis=-1, keepdims=True)).astype(jnp.bfloat16)
        mixed = jnp.einsum("hqk,khe->qhe", attn_probs, values, preferred_element_type=jnp.float32)
        return mixed.astype(jnp.bfloat16)

    attended = lax.map(attend, (query_rows, query_segs)).reshape(all_rows, head_cols)
    out_full = lax.all_gather(w_out, "tok", axis=1, tiled=True)
    attn_rows = lax.psum_scatter(
        jnp.dot(attended, out_full, preferred_element_type=jnp.float32).astype(jnp.bfloat16),
        "blk",
        scatter_dimension=0,
        tiled=True,
    ).astype(jnp.float32)
    after_attn = tok_block.astype(jnp.float32) + attn_rows + out_bias
    normed_two = layer_norm(after_attn, ln2_gain, ln2_bias).astype(jnp.bfloat16)
    pre_act = (
        jnp.dot(
            lax.all_gather(normed_two, "blk", axis=0, tiled=True),
            w_fc1,
            preferred_element_type=jnp.float32,
        )
        + fc1_bias
    )
    hidden_act = jax.nn.gelu(pre_act, approximate=False).astype(jnp.bfloat16)
    partial_sum = jnp.dot(hidden_act, w_fc2, preferred_element_type=jnp.float32)
    own_start = lax.axis_index("blk") * row_count
    own_rows = lax.dynamic_slice_in_dim(partial_sum, own_start, row_count, 0) + after_attn
    partial_sum = lax.dynamic_update_slice_in_dim(partial_sum, own_rows, own_start, 0)
    summed = lax.psum(partial_sum.astype(jnp.bfloat16), "blk").astype(jnp.float32)
    layer_all = (summed + fc2_bias).astype(jnp.bfloat16)
    final_all = layer_norm(layer_all, ln3_gain, ln3_bias).astype(jnp.bfloat16)
    merge_rows = merge_index[0]
    merged_count = merge_rows.shape[0]
    merged = jnp.take(final_all, merge_rows.reshape(-1), axis=0).reshape(
        merged_count, 4 * model_width
    )
    columns = merged
    projected = jnp.dot(
        columns,
        lax.all_gather(w_proj, "tok", axis=0, tiled=True),
        preferred_element_type=jnp.float32,
    )
    projected = (projected + proj_bias).astype(jnp.bfloat16)
    tok_count = lax.axis_size("tok")
    slot_cap = 2 * merged_count // tok_count
    owners_here = segment_owner[0]
    seg_rows = jnp.take(segment_row, merge_rows[:, 0])
    seg_match = (
        seg_rows[:, None] == jnp.arange(owners_here.shape[0], dtype=jnp.int32)[None, :]
    ).astype(jnp.int32)
    owner_rows = jnp.sum(seg_match * owners_here[None, :], axis=1)
    segment_matches = (
        owner_rows[:, None] == jnp.arange(tok_count, dtype=jnp.int32)[None, :]
    ).astype(jnp.int32)
    before = jnp.cumsum(segment_matches, axis=0) - segment_matches
    order_in = jnp.sum(before * segment_matches, axis=1)
    target = owner_rows * slot_cap + order_in
    placed = (jnp.arange(tok_count * slot_cap, dtype=jnp.int32)[:, None] == target[None, :]).astype(
        jnp.bfloat16
    )
    outgoing = jnp.dot(placed, projected, preferred_element_type=jnp.float32).astype(jnp.bfloat16)
    outgoing = outgoing.reshape(tok_count, slot_cap, projected.shape[1])
    arrived = lax.all_to_all(outgoing, "tok", split_axis=0, concat_axis=0, tiled=True)
    return arrived[None]


def solution(mesh):
    placed = (
        P("tok", "blk", None),
        P("tok", None),
        P("tok", None, None),
        P("tok", None),
        P(),
        P(),
        P(None, "tok", "blk"),
        P(None, "blk"),
        P("blk", "tok"),
        P(),
        P(),
        P(),
        P(None, "blk"),
        P("blk"),
        P("blk", None),
        P(),
        P(),
        P(),
        P("tok", "blk"),
        P("blk"),
    )
    return jax.shard_map(
        body, mesh=mesh, in_specs=placed, out_specs=P("tok", None, None, "blk"), check_vma=False
    )
```

profile of v0, /device:TPU:1, one launch (start us, length us, event | category | flops | bytes accessed | tf_op | source)
XLA Modules:
  0.0 480.8 jit_solution(5821261523930769322)
XLA Ops:
  6.5 0.7 all-gather.15.cloned.1.call-update
  7.3 1.3 convert_reduce_fusion.1
  8.7 1.5 fusion.43
  10.2 2.5 fusion.46
  12.8 1.7 copy.32
  14.6 0.5 broadcast.197
  15.1 1.3 reduce.6
  16.4 40.5 %all-gather.15.cloned.1.call-done = bf16[32,52,416]{2,1,0:T(8,128)(2,1)} async-done(((bf16[1,52,416]{2,1,0:T(8,128)(2,1)}), bf16[32,52,416]{2,1,0:T(8,128)(2,1)}) %all-gather.15.cloned.1.call-update) | async-done | bytes 1384464 | tf_op jit(solution)/shard_map/all_gather | solution.py:79
  56.9 2.7 reshape.179
  59.7 39.4 %all-gather.7.cloned.1.call-done = bf16[1024,1664]{1,0:T(8,128)(2,1)} async-done(((bf16[256,1664]{1,0:T(8,128)(2,1)}), bf16[1024,1664]{1,0:T(8,128)(2,1)}) %all-gather.7.cloned.1.call-update) | async-done | bytes 3407888 | tf_op jit(solution)/shard_map/all_gather | solution.py:46
  99.1 53.1 %all-gather.9.cloned.1.call-done = bf16[3,1664,416]{2,0,1:T(4,128)(2,1)} async-done(((bf16[3,52,416]{2,0,1:T(4,128)(2,1)}), bf16[3,1664,416]{2,0,1:T(4,128)(2,1)}) %all-gather.9.cloned.1.call-update) | async-done | bytes 4153360 | tf_op jit(solution)/shard_map/all_gather | solution.py:52
  152.2 9.2 %fusion.34 = bf16[3,1024,416]{1,2,0:T(8,128)(2,1)S(1)} fusion(f32[3,416]{1,0:T(4,128)S(1)} %copy-done.15, bf16[3,1664,416]{2,0,1:T(4,128)(2,1)} %all-gather.9.cloned.1.call-done, bf16[1024,1664]{1,0:T(8,128)(2,1)} %all-gather.7.cloned.1.call-done), kind=kOutput, calls=%fused_computation.53 | convolution fusion | flops 4255580160 | bytes 10122112 | tf_op jit(solution)/shard_map/td,cde->cte/dot_general | solution.py:49
  161.4 1.4 fusion.96
  162.8 0.6 reshape_squeeze.10
  163.4 1.0 copy.34
  164.4 15.8 %while.10 = (s32[]{:T(128)}, bf16[2,512,4,104]{1,3,2,0:T(8,128)(2,1)}, s32[2,512]{1,0:T(2,128)S(1)}, s32[1,1024]{1,0:T(1,128)S(1)}, bf16[2,512,4,104]{1,3,2,0:T(...) while((s32[]{:T(128)}, bf16[2,512,4,104]{1,3,2,0:T(8,128)(2,1)}, ...), condition=%wide.region_8.9_spmd, body=%wide.region_6.8_spmd.sunk | while | flops 887830528 | bytes 31156912 | solution.py:78
  164.8 4.0 fusion.112
  168.8 2.5 fusion.113
  171.3 0.9 copy-done.6
  172.6 4.0 fusion.112
  176.6 2.5 fusion.113
  179.2 0.9 copy-done.6
  180.2 2.0 copy.35
  182.4 3.9 convolution_convert_fusion
  186.4 38.9 %reduce-scatter.2.cloned.1.call-done = bf16[256,1664]{1,0:T(8,128)(2,1)} async-done(((bf16[1024,1664]{1,0:T(8,128)(2,1)}), bf16[256,1664]{1,0:T(8,128)(2,1)}) %reduce-scatter.2.cloned.1.call-update) | async-done | bytes 851984 | tf_op jit(solution)/shard_map/reduce_scatter | solution.py:80
  225.3 1.5 fusion.57
  226.9 1.7 multiply_reduce_fusion
  228.5 2.6 add_convert_fusion.2
  231.3 41.5 %all-gather.11.cloned.1.call-done = bf16[1024,1664]{1,0:T(8,128)(2,1)} async-done(((bf16[256,1664]{1,0:T(8,128)(2,1)}), bf16[1024,1664]{1,0:T(8,128)(2,1)}) %all-gather.11.cloned.1.call-update) | async-done | bytes 3407888 | tf_op jit(solution)/shard_map/all_gather | solution.py:90
  272.7 11.1 %fusion.97 = f32[1024,2048]{1,0:T(8,128)S(1)} fusion(bf16[1024,1664]{1,0:T(8,128)(2,1)} %all-gather.11.cloned.1.call-done, bf16[1664,2048]{1,0:T(8,128)(2,1)} %param.34), kind=kOutput, calls=%fused_computation.133 | convolution fusion | flops 6979321856 | bytes 18612224 | tf_op jit(solution)/shard_map/dot_general | solution.py:89
  283.9 28.8 %fusion.29 = f32[1024,1664]{1,0:T(8,128)S(1)} fusion(bf16[2048,1664]{1,0:T(8,128)(2,1)} %param.36, f32[1024,2048]{1,0:T(8,128)S(1)} %fusion.97, f32[2048]{0:T(1024)S(1)} %copy-done.16), kind=kOutput, calls=%fused_computation.48 | convolution fusion | flops 7117733888 | bytes 22028288 | tf_op jit(solution)/shard_map/dot_general | solution.py:97
  313.2 2.2 convert_element_type.78
  315.5 0.7 all-gather.13.cloned.1.call-update
  316.5 1.4 gather_fusion
  318.0 0.6 reduce-window.6
  319.0 0.9 broadcast_in_dim.40
  320.0 2.0 copy.39
  322.1 73.7 %all-reduce.2.cloned.1.call-done = bf16[1024,1664]{1,0:T(8,128)(2,1)} async-done(((bf16[1024,1664]{1,0:T(8,128)(2,1)}), bf16[1024,1664]{1,0:T(8,128)(2,1)}) %all-reduce.2.cloned.1.call-update) | async-done | bytes 3407888 | tf_op jit(solution)/shard_map/psum | solution.py:101
  395.8 2.8 convert_reduce_fusion
  398.7 3.2 fusion.23
  401.9 1.8 fusion.26
  403.7 5.9 %gather_fusion.1 = bf16[1024,1664]{1,0:T(8,128)(2,1)} fusion(bf16[1024,1664]{1,0:T(8,128)(2,1)S(1)} %fusion.26, s32[1024]{0:T(1024)S(1)} %broadcast_clamp_fusion), kind=kCustom, calls=%fused_computation.1 | custom fusion | bytes 6819840 | tf_op jit(solution)/shard_map/jit(_take)/gather | solution.py:106
  409.6 5.4 %gather.15 = bf16[256,6656]{1,0:T(8,128)(2,1)S(1)} reshape(bf16[1024,1664]{1,0:T(8,128)(2,1)} %gather_fusion.1) | data formatting | bytes 6815744 | tf_op jit(solution)/shard_map/jit(_take)/gather | solution.py:106
  415.0 33.5 %all-gather.13.cloned.1.call-done = bf16[6656,416]{1,0:T(8,128)(2,1)} async-done(((bf16[208,416]{1,0:T(8,128)(2,1)}), bf16[6656,416]{1,0:T(8,128)(2,1)}) %all-gather.13.cloned.1.call-update) | async-done | bytes 5537808 | tf_op jit(solution)/shard_map/all_gather | solution.py:112
  448.5 7.0 %convolution_convert_fusion.1 = bf16[512,416]{0,1:T(8,128)(2,1)} fusion(bf16[6656,416]{1,0:T(8,128)(2,1)} %all-gather.13.cloned.1.call-done, pred[256,6656]{1,0:T(8,128)(4,1)} %bitcast.118, bf16[256,6656]{1,0:T(8,128)(2,1)S(1)} %gather.15, s32[256]{0:T(256)S(1)} %multiply_add_fusion, f32[416]{0:T(512)S(1)} %copy-done.17), kind=kOutput, calls=%fused_computation.69 | convolution fusion | flops 1528987648 | bytes 11078272 | tf_op jit(solution)/shard_map/dot_general | solution.py:133
  455.5 1.2 copy.37
  456.7 16.2 %all_to_all.5 = bf16[32,16,416]{2,1,0:T(8,128)(2,1)S(1)} all-to-all(bf16[32,16,416]{2,1,0:T(8,128)(2,1)S(1)} %bitcast.116), channel_id=1, replica_groups=mesh['blk'=4,'tok'=32] {'tok'}, dimensions={0} | all-to-all | bytes 851968 | tf_op jit(solution)/shard_map/all_to_all | solution.py:135
  472.9 0.8 copy.56
  (82 shorter events, 2.7 us)
Async XLA Ops:
  6.5 145.7 %copy-start.15 = (f32[3,416]{1,0:T(4,128)S(1)}, f32[3,416]{1,0:T(4,128)}, u32[]{:S(2)}) copy-start(f32[3,416]{1,0:T(4,128)} %param.29) | copy-start | bytes 14980
  6.5 50.4 %all-gather.15.cloned.1.call-start = ((), (), s32[]{:S(2)}) async-start(), calls=%async_computation.8 | async-start | bytes 1892352 | tf_op jit(solution)/shard_map/all_gather | solution.py:79
  7.3 91.8 %all-gather.7.cloned.1.call-start = ((), (), s32[]{:S(2)}) async-start(), calls=%async_computation.2 | async-start | bytes 4259840 | tf_op jit(solution)/shard_map/all_gather | solution.py:46
  12.8 139.4 %all-gather.9.cloned.1.call-start = ((), (), s32[]{:S(2)}) async-start(), calls=%async_computation.3 | async-start | bytes 7028736 | tf_op jit(solution)/shard_map/all_gather | solution.py:52
  14.5 210.8 %reduce-scatter.2.cloned.1.call-start = ((), (), s32[]{:S(2)}) async-start(), calls=%async_computation.4 | async-start | bytes 4259840 | tf_op jit(solution)/shard_map/reduce_scatter | solution.py:80
  161.4 3.0 copy-start
  164.4 4.3 copy-start.4
  164.4 4.3 copy-start.5
  171.3 0.9 copy-start.6
  172.2 4.3 copy-start.4
  172.2 4.3 copy-start.5
  179.1 0.9 copy-start.6
  182.4 42.9 %copy-start.1 = (bf16[1,256,1664]{2,1,0:T(8,128)(2,1)S(1)}, bf16[1,256,1664]{2,1,0:T(8,128)(2,1)}, u32[]{:S(2)}) copy-start(bf16[1,256,1664]{2,1,0:T(8,128)(2,1)} %param.22) | copy-start | bytes 2555908
  182.4 42.9 %copy-start.7 = (f32[1664]{0:T(1024)S(1)}, f32[1664]{0:T(1024)}, u32[]{:S(2)}) copy-start(f32[1664]{0:T(1024)} %param.31) | copy-start | bytes 19972
  186.4 42.2 %copy-start.10 = (f32[1664]{0:T(1024)S(1)}, f32[1664]{0:T(1024)}, u32[]{:S(2)}) copy-start(f32[1664]{0:T(1024)} %param.33) | copy-start | bytes 19972
  186.4 42.2 %copy-start.11 = (f32[1664]{0:T(1024)S(1)}, f32[1664]{0:T(1024)}, u32[]{:S(2)}) copy-start(f32[1664]{0:T(1024)} %param.32) | copy-start | bytes 19972
  186.4 86.3 %all-gather.11.cloned.1.call-start = ((), (), s32[]{:S(2)}) async-start(), calls=%async_computation.5 | async-start | bytes 4259840 | tf_op jit(solution)/shard_map/all_gather | solution.py:90
  231.2 164.6 %all-reduce.2.cloned.1.call-start = ((), (), s32[]{:S(2)}) async-start(), calls=%async_computation.6 | async-start | bytes 6815744 | tf_op jit(solution)/shard_map/psum | solution.py:101
  231.2 52.6 %copy-start.16 = (f32[2048]{0:T(1024)S(1)}, f32[2048]{0:T(1024)}, u32[]{:S(2)}) copy-start(f32[2048]{0:T(1024)} %param.35) | copy-start | bytes 24580
  283.9 28.9 %copy-start.3 = (bf16[256,1664]{1,0:T(8,128)(2,1)S(1)}, bf16[256,1664]{1,0:T(8,128)(2,1)}, u32[]{:S(2)}) copy-start(bf16[256,1664]{1,0:T(8,128)(2,1)} %reduce-scatter.2.cloned.1.call-done) | copy-start | bytes 2555908
  313.2 3.0 copy-start.9
  313.2 4.7 copy-start.14
  315.4 80.4 %copy-start.8 = (f32[1664]{0:T(1024)S(1)}, f32[1664]{0:T(1024)}, u32[]{:S(2)}) copy-start(f32[1664]{0:T(1024)} %param.37) | copy-start | bytes 19972
  315.4 133.1 %all-gather.13.cloned.1.call-start = ((), (), s32[]{:S(2)}) async-start(), calls=%async_computation.7 | async-start | bytes 7028736 | tf_op jit(solution)/shard_map/all_gather | solution.py:112
  316.2 85.7 %copy-start.12 = (f32[1664]{0:T(1024)S(1)}, f32[1664]{0:T(1024)}, u32[]{:S(2)}) copy-start(f32[1664]{0:T(1024)} %param.39) | copy-start | bytes 19972
  316.2 85.6 %copy-start.13 = (f32[1664]{0:T(1024)S(1)}, f32[1664]{0:T(1024)}, u32[]{:S(2)}) copy-start(f32[1664]{0:T(1024)} %param.38) | copy-start | bytes 19972
  395.8 6.1 %copy-start.2 = (bf16[1024,1664]{1,0:T(8,128)(2,1)S(1)}, bf16[1024,1664]{1,0:T(8,128)(2,1)}, u32[]{:S(2)}) copy-start(bf16[1024,1664]{1,0:T(8,128)(2,1)} %all-reduce.2.cloned.1.call-done) | copy-start | bytes 10223620
  409.6 39.0 %copy-start.17 = (f32[416]{0:T(512)S(1)}, f32[416]{0:T(512)}, u32[]{:S(2)}) copy-start(f32[416]{0:T(512)} %param.41) | copy-start | bytes 4996
Sparse Core Ops, SparseCore 0:
  9.6 47.2 all-gather.14
  58.6 40.4 all-gather.6
  101.3 50.8 all-gather.8
  186.5 38.7 reduce-scatter.1
  231.3 41.3 all-gather.10
  315.5 80.1 all-reduce.1
  398.0 50.4 all-gather.12
where the time goes:
time: 490 us; the launch traced here: 481 us
  waiting for transfers between devices  322 us (66%)
  matrix products  73 us (15%)
  local copies, waits for them, and re-layouts  30.3 us (6%)
  other arithmetic  24.6 us (5%)
  blocking collectives  16.2 us (3%)
  between operations  14 us (3%)
    psum x1, waiting for transfers between devices, body(): lax.psum(partial_sum.astype(jnp.bfloat16), 'blk').astype(jnp.float32)  73.7 us
    all_gather x1, waiting for transfers between devices, body(): lax.all_gather(w_qkv, 'tok', axis=1, tiled=True)  53.1 us
    all_gather x1, waiting for transfers between devices, body(): lax.all_gather(normed_two, 'blk', axis=0, tiled=True)  41.5 us
    all_gather x1, waiting for transfers between devices, body(): out_full = lax.all_gather(w_out, 'tok', axis=1, tiled=True)  40.5 us
    all_gather x1, waiting for transfers between devices, body(): normed_all = lax.all_gather(normed_one, 'blk', axis=0, tiled=True)  39.4 us
    reduce_scatter x1, waiting for transfers between devices, body(): lax.psum_scatter(jnp.dot(attended, out_full, preferred_element_type=jnp.f...  38.9 us
    all_gather x1, waiting for transfers between devices, body(): lax.all_gather(w_proj, 'tok', axis=0, tiled=True)  33.5 us
    dot_general x1, matrix products, body(): partial_sum = jnp.dot(hidden_act, w_fc2, preferred_element_type=jnp.float32)  28.8 us
  transfers between devices with their start and end apart: 7, of which 7 were waited for; matrix products, arithmetic and copies ran while one was open for 8% of the time, Pallas kernels for 0%

commit v1 on v0

--- a/solution.py
+++ b/solution.py
@@ -43,7 +43,14 @@
     head_cols = w_qkv.shape[2]
     heads_here = head_cols // HD
     normed_one = layer_norm(tok_block, ln1_gain, ln1_bias).astype(jnp.bfloat16)
-    normed_all = lax.all_gather(normed_one, "blk", axis=0, tiled=True)
+    peers = lax.axis_size("blk")
+    route = [(i, (i + 1) % peers) for i in range(peers)]
+    parts = [normed_one]
+    for reach in range(1, peers):
+        parts = [lax.ppermute(parts[0], "blk", route), *parts]
+    whole = jnp.concatenate(parts, axis=0)
+    shift = (lax.axis_index("blk") + 1) * parts[-1].shape[0]
+    normed_all = jnp.roll(whole, shift, axis=0)
     all_rows = normed_all.shape[0]
     columns = normed_all
     projected_qkv = jnp.einsum(

time: 490 us -> 439 us (0.90); the launches traced: 481 us -> 436 us
  waiting for transfers between devices: 322 us -> 267 us
  local copies, waits for them, and re-layouts: 30.3 us -> 35.3 us
    ppermute x0 -> x3, waiting for transfers between devices: none -> 56.7 us  [body(): parts = [lax.ppermute(parts[0], 'blk', route), *parts]]
    all_gather x1, waiting for transfers between devices: 40.5 us -> 0.01 us  [body(): out_full = lax.all_gather(w_out, 'tok', axis=1, tiled=True)]
    all_gather x1 -> x0, waiting for transfers between devices: 39.4 us -> none  [body(): normed_all = lax.all_gather(normed_one, 'blk', axis=0, tiled=True)]
    all_gather x1, waiting for transfers between devices: 53.1 us -> 21.4 us  [body(): lax.all_gather(w_qkv, 'tok', axis=1, tiled=True)]
    unnamed x37 -> x49, local copies, waits for them, and re-layouts: 8.1 us -> 15.2 us
  transfers between devices with their start and end apart: 7 -> 9, of which waited for: 7 -> 8; matrix products, arithmetic and copies ran while one was open for 8% -> 10% of each run, Pallas kernels for 0% -> 0%
where the time goes in v1:
time: 439 us; the launch traced here: 436 us
  waiting for transfers between devices  267 us (61%)
  matrix products  74.3 us (17%)
  local copies, waits for them, and re-layouts  35.3 us (8%)
  other arithmetic  26.3 us (6%)
  blocking collectives  16.2 us (4%)
  between operations  14.1 us (3%)
    psum x1, waiting for transfers between devices, body(): lax.psum(partial_sum.astype(jnp.bfloat16), 'blk').astype(jnp.float32)  73.9 us
    ppermute x3, waiting for transfers between devices, body(): parts = [lax.ppermute(parts[0], 'blk', route), *parts]  56.7 us
    all_gather x1, waiting for transfers between devices, body(): lax.all_gather(normed_two, 'blk', axis=0, tiled=True)  41.5 us
    reduce_scatter x1, waiting for transfers between devices, body(): lax.psum_scatter(jnp.dot(attended, out_full, preferred_element_type=jnp.f...  38.9 us
    all_gather x1, waiting for transfers between devices, body(): lax.all_gather(w_proj, 'tok', axis=0, tiled=True)  33.4 us
    dot_general x1, matrix products, body(): partial_sum = jnp.dot(hidden_act, w_fc2, preferred_element_type=jnp.float32)  28.6 us
    all_gather x1, waiting for transfers between devices, body(): lax.all_gather(w_qkv, 'tok', axis=1, tiled=True)  21.4 us
    all_to_all x1, blocking collectives, body(): lax.all_to_all(outgoing, 'tok', split_axis=0, concat_axis=0, tiled=True)  16.2 us
  transfers between devices with their start and end apart: 9, of which 8 were waited for; matrix products, arithmetic and copies ran while one was open for 10% of the time, Pallas kernels for 0%

profile of v1, /device:TPU:1, one launch (start us, length us, event | category | flops | bytes accessed | tf_op | source)
XLA Modules:
  0.0 436.2 jit_solution(14914839660769495858)
XLA Ops:
  7.3 1.7 copy.32
  9.1 1.3 convert_reduce_fusion.1
  10.5 1.5 fusion.44
  12.0 1.6 fusion.47
  13.6 2.1 collective-permute-start
  15.7 19.6 %collective-permute-done = bf16[256,1664]{1,0:T(8,128)(2,1)S(1)} collective-permute-done((bf16[256,1664]{1,0:T(8,128)(2,1)S(1)}, bf16[256,1664]{1,0:T(8,128)(2,1)S(1)}, u32[]{:S(2)}, u32[]{:S(2)}) %collective-permute-start) | collective-permute-done | bytes 852000 | tf_op jit(solution)/shard_map/ppermute | solution.py:50
  35.6 19.8 %collective-permute-done.1 = bf16[256,1664]{1,0:T(8,128)(2,1)S(1)} collective-permute-done((bf16[256,1664]{1,0:T(8,128)(2,1)S(1)}, bf16[256,1664]{1,0:T(8,128)(2,1)S(1)}, u32[]{:S(2)}, u32[]{:S(2)}) %collective-permute-start.1) | collective-permute-done | bytes 852000 | tf_op jit(solution)/shard_map/ppermute | solution.py:50
  56.1 1.3 reduce.6
  57.4 17.3 %collective-permute-done.2 = bf16[256,1664]{1,0:T(8,128)(2,1)S(1)} collective-permute-done((bf16[256,1664]{1,0:T(8,128)(2,1)S(1)}, bf16[256,1664]{1,0:T(8,128)(2,1)S(1)}, u32[]{:S(2)}, u32[]{:S(2)}) %collective-permute-start.2) | collective-permute-done | bytes 852000 | tf_op jit(solution)/shard_map/ppermute | solution.py:50
  74.7 1.0 constant_dynamic-update-slice_fusion.7
  75.6 1.0 constant_dynamic-update-slice_fusion.6
  76.7 1.0 constant_dynamic-update-slice_fusion.5
  77.7 1.3 constant_dynamic-update-slice_fusion.4
  79.0 1.0 constant_dynamic-update-slice_fusion.3
  80.9 1.0 constant_dynamic-update-slice_fusion.1
  81.9 1.4 constant_dynamic-update-slice_fusion
  83.3 3.9 reshape.179
  87.2 21.4 %all-gather.6.cloned.1.call-done = bf16[3,1664,416]{2,0,1:T(4,128)(2,1)} async-done(((bf16[3,52,416]{2,0,1:T(4,128)(2,1)}), bf16[3,1664,416]{2,0,1:T(4,128)(2,1)}) %all-gather.6.cloned.1.call-update) | async-done | bytes 4153360 | tf_op jit(solution)/shard_map/all_gather | solution.py:59
  108.6 9.2 %fusion.35 = bf16[3,1024,416]{1,2,0:T(8,128)(2,1)S(1)} fusion(f32[3,416]{1,0:T(4,128)S(1)} %copy-done.15, bf16[3,1664,416]{2,0,1:T(4,128)(2,1)} %all-gather.6.cloned.1.call-done, bf16[2048,1664]{1,0:T(8,128)(2,1)} %constant_dynamic-update-slice_fusion, s32[]{:T(128)S(6)} %select_n.59), kind=kOutput, calls=%fused_computation.54 | convolution fusion | flops 4255580160 | bytes 12784516 | tf_op jit(solution)/shard_map/td,cde->cte/dot_general | solution.py:56
  117.8 1.1 fusion.98
  119.5 1.0 copy.34
  120.5 15.2 %while.10 = (s32[]{:T(128)}, bf16[2,512,4,104]{1,3,2,0:T(8,128)(2,1)}, s32[2,512]{1,0:T(2,128)S(1)}, s32[1,1024]{1,0:T(1,128)S(1)}, bf16[2,512,4,104]{1,3,2,0:T(...) while((s32[]{:T(128)}, bf16[2,512,4,104]{1,3,2,0:T(8,128)(2,1)}, ...), condition=%wide.region_8.9_spmd, body=%wide.region_6.8_spmd.sunk | while | flops 887830528 | bytes 20933720 | solution.py:85
  120.9 4.0 fusion.114
  124.9 3.2 fusion.115
  128.5 3.8 fusion.114
  132.3 3.2 fusion.115
  135.7 2.0 copy.35
  138.0 3.9 convolution_convert_fusion
  142.0 38.9 %reduce-scatter.2.cloned.1.call-done = bf16[256,1664]{1,0:T(8,128)(2,1)} async-done(((bf16[1024,1664]{1,0:T(8,128)(2,1)}), bf16[256,1664]{1,0:T(8,128)(2,1)}) %reduce-scatter.2.cloned.1.call-update) | async-done | bytes 851984 | tf_op jit(solution)/shard_map/reduce_scatter | solution.py:87
  180.9 1.5 fusion.58
  182.4 1.7 multiply_reduce_fusion
  184.1 2.6 add_convert_fusion.2
  186.8 41.5 %all-gather.8.cloned.1.call-done = bf16[1024,1664]{1,0:T(8,128)(2,1)} async-done(((bf16[256,1664]{1,0:T(8,128)(2,1)}), bf16[1024,1664]{1,0:T(8,128)(2,1)}) %all-gather.8.cloned.1.call-update) | async-done | bytes 3407888 | tf_op jit(solution)/shard_map/all_gather | solution.py:97
  228.3 11.3 %fusion.99 = f32[1024,2048]{1,0:T(8,128)S(1)} fusion(bf16[1024,1664]{1,0:T(8,128)(2,1)} %all-gather.8.cloned.1.call-done, bf16[1664,2048]{1,0:T(8,128)(2,1)} %param.34), kind=kOutput, calls=%fused_computation.143 | convolution fusion | flops 6979321856 | bytes 18612224 | tf_op jit(solution)/shard_map/dot_general | solution.py:96
  239.6 28.6 %fusion.29 = f32[1024,1664]{1,0:T(8,128)S(1)} fusion(bf16[2048,1664]{1,0:T(8,128)(2,1)} %param.36, f32[1024,2048]{1,0:T(8,128)S(1)} %fusion.99, f32[2048]{0:T(1024)S(1)} %copy-done.16), kind=kOutput, calls=%fused_computation.48 | convolution fusion | flops 7117733888 | bytes 22028288 | tf_op jit(solution)/shard_map/dot_general | solution.py:104
  268.8 2.2 convert_element_type.78
  271.9 1.4 gather_fusion
  275.4 2.0 copy.39
  277.5 73.9 %all-reduce.2.cloned.1.call-done = bf16[1024,1664]{1,0:T(8,128)(2,1)} async-done(((bf16[1024,1664]{1,0:T(8,128)(2,1)}), bf16[1024,1664]{1,0:T(8,128)(2,1)}) %all-reduce.2.cloned.1.call-update) | async-done | bytes 3407888 | tf_op jit(solution)/shard_map/psum | solution.py:108
  351.3 2.8 convert_reduce_fusion
  354.2 3.2 fusion.23
  357.4 1.8 fusion.26
  359.3 5.9 %gather_fusion.1 = bf16[1024,1664]{1,0:T(8,128)(2,1)} fusion(bf16[1024,1664]{1,0:T(8,128)(2,1)S(1)} %fusion.26, s32[1024]{0:T(1024)S(1)} %broadcast_clamp_fusion), kind=kCustom, calls=%fused_computation.1 | custom fusion | bytes 6819840 | tf_op jit(solution)/shard_map/jit(_take)/gather | solution.py:113
  365.1 5.4 %gather.15 = bf16[256,6656]{1,0:T(8,128)(2,1)S(1)} reshape(bf16[1024,1664]{1,0:T(8,128)(2,1)} %gather_fusion.1) | data formatting | bytes 6815744 | tf_op jit(solution)/shard_map/jit(_take)/gather | solution.py:113
  370.6 33.4 %all-gather.10.cloned.1.call-done = bf16[6656,416]{1,0:T(8,128)(2,1)} async-done(((bf16[208,416]{1,0:T(8,128)(2,1)}), bf16[6656,416]{1,0:T(8,128)(2,1)}) %all-gather.10.cloned.1.call-update) | async-done | bytes 5537808 | tf_op jit(solution)/shard_map/all_gather | solution.py:119
  403.9 7.0 %convolution_convert_fusion.1 = bf16[512,416]{0,1:T(8,128)(2,1)} fusion(bf16[6656,416]{1,0:T(8,128)(2,1)} %all-gather.10.cloned.1.call-done, pred[256,6656]{1,0:T(8,128)(4,1)} %bitcast.122, bf16[256,6656]{1,0:T(8,128)(2,1)S(1)} %gather.15, s32[256]{0:T(256)S(1)} %multiply_add_fusion, f32[416]{0:T(512)S(1)} %copy-done.17), kind=kOutput, calls=%fused_computation.70 | convolution fusion | flops 1528987648 | bytes 11078272 | tf_op jit(solution)/shard_map/dot_general | solution.py:140
  410.9 1.2 copy.37
  412.1 16.2 %all_to_all.5 = bf16[32,16,416]{2,1,0:T(8,128)(2,1)S(1)} all-to-all(bf16[32,16,416]{2,1,0:T(8,128)(2,1)S(1)} %bitcast.120), channel_id=1, replica_groups=mesh['blk'=4,'tok'=32] {'tok'}, dimensions={0} | all-to-all | bytes 851968 | tf_op jit(solution)/shard_map/all_to_all | solution.py:142
  (87 shorter events, 8.8 us)
Async XLA Ops:
  6.5 71.2 %copy-start.1 = (bf16[1,256,1664]{2,1,0:T(8,128)(2,1)S(1)}, bf16[1,256,1664]{2,1,0:T(8,128)(2,1)}, u32[]{:S(2)}) copy-start(bf16[1,256,1664]{2,1,0:T(8,128)(2,1)} %param.22) | copy-start | bytes 2555908
  6.5 71.2 %copy-start.7 = (f32[1664]{0:T(1024)S(1)}, f32[1664]{0:T(1024)}, u32[]{:S(2)}) copy-start(f32[1664]{0:T(1024)} %param.26) | copy-start | bytes 19972
  6.5 71.2 %copy-start.6 = (f32[1664]{0:T(1024)S(1)}, f32[1664]{0:T(1024)}, u32[]{:S(2)}) copy-start(f32[1664]{0:T(1024)} %param.27) | copy-start | bytes 19972
  6.5 76.8 %all-gather.12.cloned.1.call-start = ((), (), s32[]{:S(2)}) async-start(), calls=%async_computation.7 | async-start | bytes 1892352 | tf_op jit(solution)/shard_map/all_gather | solution.py:86
  7.3 101.3 %all-gather.6.cloned.1.call-start = ((), (), s32[]{:S(2)}) async-start(), calls=%async_computation.2 | async-start | bytes 7028736 | tf_op jit(solution)/shard_map/all_gather | solution.py:59
  9.0 171.8 %reduce-scatter.2.cloned.1.call-start = ((), (), s32[]{:S(2)}) async-start(), calls=%async_computation.3 | async-start | bytes 4259840 | tf_op jit(solution)/shard_map/reduce_scatter | solution.py:87
  13.6 21.7 %collective-permute-start = (bf16[256,1664]{1,0:T(8,128)(2,1)S(1)}, bf16[256,1664]{1,0:T(8,128)(2,1)S(1)}, u32[]{:S(2)}, u32[]{:S(2)}) collective-permute-start(bf16[256,1664]{1,0:T(8,128)(2,1)S(1)} %fusion.47), channel_id=1, source_target_pairs={{0,32},{32,64},{64,96},{96,0},{1,33},{33,65},{65,97},{97,1},{2,34}... | collective-permute-start | bytes 2555912 | tf_op jit(solution)/shard_map/ppermute | solution.py:50
  35.3 20.1 %collective-permute-start.1 = (bf16[256,1664]{1,0:T(8,128)(2,1)S(1)}, bf16[256,1664]{1,0:T(8,128)(2,1)S(1)}, u32[]{:S(2)}, u32[]{:S(2)}) collective-permute-start(bf16[256,1664]{1,0:T(8,128)(2,1)S(1)} %collective-permute-done), channel_id=1, source_target_pairs={{0,32},{32,64},{64,96},{96,0},{1,33},{33,65},{65,97},{97,1},{2,34}... | collective-permute-start | bytes 2555912 | tf_op jit(solution)/shard_map/ppermute | solution.py:50
  55.4 19.3 %collective-permute-start.2 = (bf16[256,1664]{1,0:T(8,128)(2,1)S(1)}, bf16[256,1664]{1,0:T(8,128)(2,1)S(1)}, u32[]{:S(2)}, u32[]{:S(2)}) collective-permute-start(bf16[256,1664]{1,0:T(8,128)(2,1)S(1)} %collective-permute-done.1), channel_id=1, source_target_pairs={{0,32},{32,64},{64,96},{96,0},{1,33},{33,65},{65,97},{97,1},{2,34}... | collective-permute-start | bytes 2555912 | tf_op jit(solution)/shard_map/ppermute | solution.py:50
  76.7 31.9 %copy-start.15 = (f32[3,416]{1,0:T(4,128)S(1)}, f32[3,416]{1,0:T(4,128)}, u32[]{:S(2)}) copy-start(f32[3,416]{1,0:T(4,128)} %param.29) | copy-start | bytes 14980
  117.8 2.8 copy-start
  120.5 17.4 %copy-start.4 = (bf16[1664,416]{1,0:T(8,128)(2,1)S(1)}, bf16[1664,416]{1,0:T(8,128)(2,1)}, u32[]{:S(2)}) copy-start(bf16[1664,416]{1,0:T(8,128)(2,1)} %reshape.179) | copy-start | bytes 4153348
  138.0 42.9 %copy-start.5 = (f32[1664]{0:T(1024)S(1)}, f32[1664]{0:T(1024)}, u32[]{:S(2)}) copy-start(f32[1664]{0:T(1024)} %param.31) | copy-start | bytes 19972
  141.9 42.2 %copy-start.10 = (f32[1664]{0:T(1024)S(1)}, f32[1664]{0:T(1024)}, u32[]{:S(2)}) copy-start(f32[1664]{0:T(1024)} %param.33) | copy-start | bytes 19972
  141.9 42.2 %copy-start.11 = (f32[1664]{0:T(1024)S(1)}, f32[1664]{0:T(1024)}, u32[]{:S(2)}) copy-start(f32[1664]{0:T(1024)} %param.32) | copy-start | bytes 19972
  141.9 86.3 %all-gather.8.cloned.1.call-start = ((), (), s32[]{:S(2)}) async-start(), calls=%async_computation.4 | async-start | bytes 4259840 | tf_op jit(solution)/shard_map/all_gather | solution.py:97
  186.7 164.6 %all-reduce.2.cloned.1.call-start = ((), (), s32[]{:S(2)}) async-start(), calls=%async_computation.5 | async-start | bytes 6815744 | tf_op jit(solution)/shard_map/psum | solution.py:108
  186.8 52.8 %copy-start.16 = (f32[2048]{0:T(1024)S(1)}, f32[2048]{0:T(1024)}, u32[]{:S(2)}) copy-start(f32[2048]{0:T(1024)} %param.35) | copy-start | bytes 24580
  239.6 28.7 %copy-start.3 = (bf16[256,1664]{1,0:T(8,128)(2,1)S(1)}, bf16[256,1664]{1,0:T(8,128)(2,1)}, u32[]{:S(2)}) copy-start(bf16[256,1664]{1,0:T(8,128)(2,1)} %reduce-scatter.2.cloned.1.call-done) | copy-start | bytes 2555908
  268.7 2.8 copy-start.9
  268.8 4.5 %copy-start.14 = (s32[1,32]{1,0:T(1,128)S(1)}, s32[1,32]{1,0:T(1,128)}, u32[]{:S(2)}) copy-start(s32[1,32]{1,0:T(1,128)} %param.25) | copy-start | bytes 388
  270.9 80.4 %copy-start.8 = (f32[1664]{0:T(1024)S(1)}, f32[1664]{0:T(1024)}, u32[]{:S(2)}) copy-start(f32[1664]{0:T(1024)} %param.37) | copy-start | bytes 19972
  271.0 133.0 %all-gather.10.cloned.1.call-start = ((), (), s32[]{:S(2)}) async-start(), calls=%async_computation.6 | async-start | bytes 7028736 | tf_op jit(solution)/shard_map/all_gather | solution.py:119
  271.6 85.8 %copy-start.12 = (f32[1664]{0:T(1024)S(1)}, f32[1664]{0:T(1024)}, u32[]{:S(2)}) copy-start(f32[1664]{0:T(1024)} %param.39) | copy-start | bytes 19972
  271.6 85.8 %copy-start.13 = (f32[1664]{0:T(1024)S(1)}, f32[1664]{0:T(1024)}, u32[]{:S(2)}) copy-start(f32[1664]{0:T(1024)} %param.38) | copy-start | bytes 19972
  351.3 6.1 %copy-start.2 = (bf16[1024,1664]{1,0:T(8,128)(2,1)S(1)}, bf16[1024,1664]{1,0:T(8,128)(2,1)}, u32[]{:S(2)}) copy-start(bf16[1024,1664]{1,0:T(8,128)(2,1)} %all-reduce.2.cloned.1.call-done) | copy-start | bytes 10223620
  365.1 38.8 %copy-start.17 = (f32[416]{0:T(512)S(1)}, f32[416]{0:T(512)}, u32[]{:S(2)}) copy-start(f32[416]{0:T(512)} %param.41) | copy-start | bytes 4996
Sparse Core Ops, SparseCore 0:
  9.6 47.2 all-gather.11
  59.1 49.3 all-gather.5
  142.1 38.7 reduce-scatter.1
  186.8 41.3 all-gather.7
  271.1 80.1 all-reduce.1
  353.4 50.4 all-gather.9
